TPU v7x, 32 devices: a whole 2x2x4 slice. The times are simulated.
32 devices in a mesh: shot: 16 (over z, y, x), tm: 2 (over core).
Axes of the slice: x: 2, y: 2, z: 4, core: 2. Of those that a mesh axis runs over, the one named last changes fastest.
Arguments:
- shot_data: float32 [32, 512, 256], P('shot', None, 'tm'), may hold values from -6 to 6
- live_mask: int32 [32, 512], P('shot'), may hold values 0 or 1
- recv_order: int32 [512], replicated, may hold values from 0 to 511, each once
- rec_taps: float32 [31], replicated, may hold values from -1 to 1
- time_taps: float32 [31], replicated, may hold values from -1 to 1
- shot_taps: float32 [31], replicated, may hold values from -1 to 1
- late_taps: float32 [31], replicated, may hold values from -1 to 1
Outputs:
- filtered: float32 [32, 512, 256], P(None, 'shot', 'tm')
Inputs may be any that keep to these rules, and one draw needn't show every extreme that they name: `recv_order`: each station appears once.
All inputs are finite; a program needn't handle non-finite values. No bound on the sum of `live_mask` on one device may be relied on, other than what follows from the above.
Results may differ from a plain program's by a relative error of at most 0.00007.
Values sent between devices are 32-bit elements; how exact they have to be, the bound alone decides.
No kernel may reach another device: no remote copies, remote signals or barrier semaphores. Data moves between devices by JAX's collectives and lax.ppermute only.
A program may use at most 64 MiB of HBM per device.

v0:
```python
import jax
import jax.numpy as jnp
from jax import lax
from jax.sharding import PartitionSpec as P


def extended(value, sides, width):
    for axis, dim in sides:
        size, length = (lax.axis_size(axis), value.shape[dim])
        up = [(i, (i + 1) % size) for i in range(size - 1)]
        down = [(j, i) for i, j in up]
        last = lax.slice_in_dim(value, length - width, length, axis=dim)
        leading = lax.slice_in_dim(value, 0, width, axis=dim)
        before = lax.ppermute(last, axis, up)
        after = lax.ppermute(leading, axis, down)
        value = jnp.concatenate([before, value, after], axis=dim)
    return value


def tap_matrix(tap_list, width_out):
    tap_count = tap_list.shape[0]
    row_index = lax.broadcasted_iota(jnp.int32, (width_out + tap_count - 1, width_out), 0)
    col_index = lax.broadcasted_iota(jnp.int32, (width_out + tap_count - 1, width_out), 1)
    offsets = row_index - col_index
    picks = lax.broadcasted_iota(jnp.int32, (tap_count,), 0)
    matches = offsets[:, :, None] == picks
    return jnp.sum(jnp.where(matches, tap_list, 0.0), axis=2)


def time_filter(padded, tap_list, width_out):
    matrix = tap_matrix(tap_list, width_out)
    leading = padded.shape[:-1]
    flat_rows = padded.reshape(-1, padded.shape[-1])
    result_rows = jnp.dot(
        flat_rows, matrix, precision=lax.Precision.HIGHEST, preferred_element_type=jnp.float32
    )
    return result_rows.reshape(leading + (width_out,))


def slide_filter(values, tap_list, along):
    tap_count = tap_list.shape[0]
    half_width = (tap_count - 1) // 2
    extent = values.shape[along]
    config = [(0, 0)] * values.ndim
    config[along] = (half_width, half_width)
    padded = jnp.pad(values, config)
    summed = jnp.zeros(values.shape, jnp.float32)
    for offset in range(tap_count):
        summed = summed + tap_list[offset] * lax.slice_in_dim(
            padded, offset, offset + extent, axis=along
        )
    return summed


def shards(shot_data, live_mask, recv_order, rec_taps, time_taps, shot_taps, late_taps):
    tap_count = time_taps.shape[0]
    half_width = (tap_count - 1) // 2
    window = shot_data.shape[2]
    alive = live_mask[:, :, None].astype(jnp.float32)
    masked = shot_data * alive
    padded = extended(masked, (("tm", 2),), half_width)
    first = time_filter(padded, time_taps, window)
    across = slide_filter(first, rec_taps, 1) * alive
    sorted_rows = jnp.take(across, recv_order, axis=1)
    groups = lax.axis_size("shot")
    split_rows = sorted_rows.reshape(
        sorted_rows.shape[0], groups, sorted_rows.shape[1] // groups, sorted_rows.shape[2]
    )
    moved = lax.all_to_all(split_rows, "shot", split_axis=1, concat_axis=0, tiled=True)
    moved = moved.reshape(moved.shape[0], moved.shape[2], moved.shape[3])
    moved = slide_filter(moved, shot_taps, 0)
    padded_late = extended(moved, (("tm", 2),), half_width)
    return time_filter(padded_late, late_taps, window)


def solution(mesh):
    placed = (P("shot", None, "tm"), P("shot", None), P(), P(), P(), P(), P())
    return jax.shard_map(
        shards, mesh=mesh, in_specs=placed, out_specs=P(None, "shot", "tm"), check_vma=False
    )
```

profile of v0, /device:TPU:0, one launch (start us, length us, event | category | flops | bytes accessed | tf_op | source)
XLA Modules:
  0.0 87.5 jit_solution(1581208439452218199)
XLA Ops:
  0.0 0.7 convert_element_type.8
  0.7 1.2 %copy.24 = f32[2,512,128]{1,2,0:T(8,128)S(1)} copy(f32[2,512,128]{2,1,0:T(8,128)} %param.7) | data formatting | bytes 1048576 | tf_op args[0]
  1.9 0.0 copy-start.2
  1.9 0.0 copy-start
  2.0 0.0 copy-start.3
  2.0 0.0 copy-start.4
  2.0 0.1 broadcast_multiply_fusion
  2.1 2.4 %collective-permute-start = (f32[2,512,15]{1,2,0:T(8,128)S(1)}, f32[2,512,15]{1,2,0:T(8,128)S(1)}, u32[]{:S(2)}, u32[]{:S(2)}) collective-permute-start(f32[2,512,15]{1,2,0:T(8,128)S(1)} %get-tuple-element.9), channel_id=1, source_target_pairs={{0,1},{2,3},{4,5},{6,7},{8,9},{10,11},{12,13},{14,15},{16,17},{18,... | collective-permute-start | bytes 184328 | tf_op jit(solution)/shard_map/ppermute | solution.py:14
  4.5 1.3 %collective-permute-start.1 = (f32[2,512,15]{1,2,0:T(8,128)S(1)}, f32[2,512,15]{1,2,0:T(8,128)S(1)}, u32[]{:S(2)}, u32[]{:S(2)}) collective-permute-start(f32[2,512,15]{1,2,0:T(8,128)S(1)} %get-tuple-element.10), channel_id=1, source_target_pairs={{1,0},{3,2},{5,4},{7,6},{9,8},{11,10},{13,12},{15,14},{17,16},{19,... | collective-permute-start | bytes 184328 | tf_op jit(solution)/shard_map/ppermute | solution.py:15
  5.8 0.0 copy-done.2
  5.8 0.0 copy-done
  5.8 0.7 fusion.142
  6.5 0.7 fusion.141
  7.3 0.1 broadcast_in_dim.31
  7.4 0.0 copy-done.3
  7.4 0.0 copy-done.4
  7.4 0.6 select_reduce_fusion
  7.9 0.0 collective-permute-done
  7.9 0.0 collective-permute-done.1
  8.0 0.7 fusion.6
  8.7 23.7 %fusion.66 = f32[2,512,128]{1,2,0:T(8,128)S(1)} fusion(f32[2,512,128]{1,2,0:T(8,128)S(1)} %fusion.6, f32[]{:T(128)} %bitcast.32, f32[]{:T(128)} %bitcast.31, f32[]{:T(128)} %bitcast.30, f32[]{:T(128)} %bitcast.29, f32[]{:T(128)} %bitcast.28, f32[]{:T(128)} %bitcast.27, f32[]{:T(128)} %bitcast.26, f32[]{:T(128)} %bitcast.25, f32[]{:T(128)} %bitcast.24, ...), kind=kLoop, calls=%fused_computation.130 | loop fusion | flops 8126464 | bytes 1052796 | tf_op jit(solution)/shard_map/mul | solution.py:63
  32.3 0.2 copy.27
  32.6 2.1 %gather_fusion = f32[512,2,128]{2,1,0:T(2,128)S(1)} fusion(f32[2,512,128]{2,0,1:T(2,128)S(1)} %copy.27, s32[1024]{0:T(1024)S(1)} %pad_clamp_fusion), kind=kCustom, calls=%fused_computation | custom fusion | bytes 1050624 | tf_op jit(solution)/shard_map/jit(_take)/gather | solution.py:64
  34.7 0.1 broadcast_select_fusion
  34.8 0.8 copy.29
  35.7 0.0 copy-start.1
  35.7 7.8 %all-to-all-start = ((f32[2,16,32,128]{3,2,0,1:T(8,128)}), f32[2,16,32,128]{3,2,0,1:T(8,128)S(1)}, u32[]{:S(2)}, u32[]{:S(2)}) async-start(f32[2,16,32,128]{3,2,0,1:T(8,128)} %copy.29), calls=%async_computation | async-start | bytes 1048576 | tf_op jit(solution)/shard_map/all_to_all | solution.py:69
  43.5 0.0 copy-done.1
  43.5 0.7 fusion.140
  44.2 0.7 fusion.139
  44.9 13.9 %all-to-all-done = f32[2,16,32,128]{3,2,0,1:T(8,128)S(1)} async-done(((f32[2,16,32,128]{3,2,0,1:T(8,128)}), f32[2,16,32,128]{3,2,0,1:T(8,128)S(1)}, u32[]{:S(2)}, u32[]{:S(2)}) %all-to-all-start) | async-done | bytes 524320 | tf_op jit(solution)/shard_map/all_to_all | solution.py:69
  58.9 21.1 %fusion.125 = f32[32,32,128]{2,1,0:T(8,128)S(1)} fusion(f32[32,32,128]{2,1,0:T(8,128)S(1)} %bitcast.75, f32[]{:T(128)} %bitcast.69, f32[]{:T(128)} %bitcast.68, f32[]{:T(128)} %bitcast.67, f32[]{:T(128)} %bitcast.66, f32[]{:T(128)} %bitcast.65, f32[]{:T(128)} %bitcast.64, f32[]{:T(128)} %bitcast.63, f32[]{:T(128)} %bitcast.62, f32[]{:T(128)} %bitcast.61, ...), kind=kLoop, calls=%fused_computation.189 | loop fusion | flops 7995392 | bytes 1048700 | tf_op jit(solution)/shard_map/add | solution.py:49
  79.9 0.2 fusion.137
  80.2 1.6 %collective-permute-start.2 = (f32[32,32,15]{2,1,0:T(8,128)S(1)}, f32[32,32,15]{2,1,0:T(8,128)S(1)}, u32[]{:S(2)}, u32[]{:S(2)}) collective-permute-start(f32[32,32,15]{2,1,0:T(8,128)S(1)} %get-tuple-element.7), channel_id=1, source_target_pairs={{0,1},{2,3},{4,5},{6,7},{8,9},{10,11},{12,13},{14,15},{16,17},{18,... | collective-permute-start | bytes 184328 | tf_op jit(solution)/shard_map/ppermute | solution.py:14
  81.7 1.3 %collective-permute-start.3 = (f32[32,32,15]{2,1,0:T(8,128)S(1)}, f32[32,32,15]{2,1,0:T(8,128)S(1)}, u32[]{:S(2)}, u32[]{:S(2)}) collective-permute-start(f32[32,32,15]{2,1,0:T(8,128)S(1)} %get-tuple-element.8), channel_id=1, source_target_pairs={{1,0},{3,2},{5,4},{7,6},{9,8},{11,10},{13,12},{15,14},{17,16},{19,... | collective-permute-start | bytes 184328 | tf_op jit(solution)/shard_map/ppermute | solution.py:15
  83.0 0.2 collective-permute-done.2
  83.2 2.3 %collective-permute-done.3 = f32[32,32,15]{2,1,0:T(8,128)S(1)} collective-permute-done((f32[32,32,15]{2,1,0:T(8,128)S(1)}, f32[32,32,15]{2,1,0:T(8,128)S(1)}, u32[]{:S(2)}, u32[]{:S(2)}) %collective-permute-start.3) | collective-permute-done | bytes 61472 | tf_op jit(solution)/shard_map/ppermute | solution.py:15
  85.5 1.9 %fusion = f32[32,32,128]{2,1,0:T(8,128)} fusion(f32[32,32,15]{2,1,0:T(8,128)S(1)} %collective-permute-done.3, f32[32,32,128]{2,1,0:T(8,128)S(1)} %fusion.125, f32[32,32,15]{2,1,0:T(8,128)S(1)} %collective-permute-done.2, f32[158,128]{1,0:T(8,128)S(1)} %get-tuple-element.5), kind=kOutput, calls=%fused_computation.64 | convolution fusion | flops 248836096 | bytes 1252352 | tf_op jit(solution)/shard_map/dot_general | solution.py:34
  (6 shorter events, 0.1 us)
Async XLA Ops:
  1.9 3.8 %copy-start.2 = (s32[512]{0:T(512)S(1)}, s32[512]{0:T(512)}, u32[]{:S(2)}) copy-start(s32[512]{0:T(512)} %param.9) | copy-start | bytes 6148
  1.9 3.9 %copy-start = (f32[31]{0:T(128)S(1)}, f32[31]{0:T(128)}, u32[]{:S(2)}) copy-start(f32[31]{0:T(128)} %param.10) | copy-start | bytes 376
  2.0 5.4 %copy-start.3 = (f32[31]{0:T(128)S(1)}, f32[31]{0:T(128)}, u32[]{:S(2)}) copy-start(f32[31]{0:T(128)} %param.13) | copy-start | bytes 376
  2.0 5.4 %copy-start.4 = (f32[31]{0:T(128)S(1)}, f32[31]{0:T(128)}, u32[]{:S(2)}) copy-start(f32[31]{0:T(128)} %param.11) | copy-start | bytes 376
  2.1 5.9 %collective-permute-start = (f32[2,512,15]{1,2,0:T(8,128)S(1)}, f32[2,512,15]{1,2,0:T(8,128)S(1)}, u32[]{:S(2)}, u32[]{:S(2)}) collective-permute-start(f32[2,512,15]{1,2,0:T(8,128)S(1)} %get-tuple-element.9), channel_id=1, source_target_pairs={{0,1},{2,3},{4,5},{6,7},{8,9},{10,11},{12,13},{14,15},{16,17},{18,... | collective-permute-start | bytes 184328 | tf_op jit(solution)/shard_map/ppermute | solution.py:14
  4.5 3.5 %collective-permute-start.1 = (f32[2,512,15]{1,2,0:T(8,128)S(1)}, f32[2,512,15]{1,2,0:T(8,128)S(1)}, u32[]{:S(2)}, u32[]{:S(2)}) collective-permute-start(f32[2,512,15]{1,2,0:T(8,128)S(1)} %get-tuple-element.10), channel_id=1, source_target_pairs={{1,0},{3,2},{5,4},{7,6},{9,8},{11,10},{13,12},{15,14},{17,16},{19,... | collective-permute-start | bytes 184328 | tf_op jit(solution)/shard_map/ppermute | solution.py:15
  35.7 7.8 %copy-start.1 = (f32[31]{0:T(128)S(1)}, f32[31]{0:T(128)}, u32[]{:S(2)}) copy-start(f32[31]{0:T(128)} %param.12) | copy-start | bytes 376
  35.7 23.2 %all-to-all-start = ((f32[2,16,32,128]{3,2,0,1:T(8,128)}), f32[2,16,32,128]{3,2,0,1:T(8,128)S(1)}, u32[]{:S(2)}, u32[]{:S(2)}) async-start(f32[2,16,32,128]{3,2,0,1:T(8,128)} %copy.29), calls=%async_computation | async-start | bytes 1048576 | tf_op jit(solution)/shard_map/all_to_all | solution.py:69
  80.2 3.1 %collective-permute-start.2 = (f32[32,32,15]{2,1,0:T(8,128)S(1)}, f32[32,32,15]{2,1,0:T(8,128)S(1)}, u32[]{:S(2)}, u32[]{:S(2)}) collective-permute-start(f32[32,32,15]{2,1,0:T(8,128)S(1)} %get-tuple-element.7), channel_id=1, source_target_pairs={{0,1},{2,3},{4,5},{6,7},{8,9},{10,11},{12,13},{14,15},{16,17},{18,... | collective-permute-start | bytes 184328 | tf_op jit(solution)/shard_map/ppermute | solution.py:14
  81.7 3.8 %collective-permute-start.3 = (f32[32,32,15]{2,1,0:T(8,128)S(1)}, f32[32,32,15]{2,1,0:T(8,128)S(1)}, u32[]{:S(2)}, u32[]{:S(2)}) collective-permute-start(f32[32,32,15]{2,1,0:T(8,128)S(1)} %get-tuple-element.8), channel_id=1, source_target_pairs={{1,0},{3,2},{5,4},{7,6},{9,8},{11,10},{13,12},{15,14},{17,16},{19,... | collective-permute-start | bytes 184328 | tf_op jit(solution)/shard_map/ppermute | solution.py:15
where the time goes:
time: 88.4 us; the launch traced here: 87.5 us
  other arithmetic  46.2 us (52%)
  waiting for transfers between devices  16.4 us (19%)
  starting transfers between devices  14.4 us (16%)
  local copies, waits for them, and re-layouts  7.59 us (9%)
  matrix products  2.65 us (3%)
    mul x1, other arithmetic, shards(): across = slide_filter(first, rec_taps, 1) * alive  23.7 us
    add x1, other arithmetic, slide_filter(): summed + tap_list[offset] * lax.slice_in_dim(padded, offset, offset + ext...  21.1 us
    all_to_all x1, waiting for transfers between devices, shards(): lax.all_to_all(split_rows, 'shot', split_axis=1, concat_axis=0, tiled=True)  13.9 us
    all_to_all x1, starting transfers between devices, shards(): lax.all_to_all(split_rows, 'shot', split_axis=1, concat_axis=0, tiled=True)  7.82 us
    ppermute x2, starting transfers between devices, extended(): before = lax.ppermute(last, axis, up)  3.98 us
    slice x4, local copies, waits for them, and re-layouts, slide_filter(): tap_list[offset]  2.84 us
    dot_general x2, matrix products, time_filter(): jnp.dot(flat_rows, matrix, precision=lax.Precision.HIGHEST, preferred_ele...  2.65 us
    ppermute x2, starting transfers between devices, extended(): after = lax.ppermute(leading, axis, down)  2.58 us
  transfers between devices with their start and end apart: 5, of which 3 were waited for; matrix products, arithmetic and copies ran while one was open for 4% of the time, Pallas kernels for 0%

commit v1 on v0

v1 whole, which is shorter than its diff:
```python
import functools

import jax
import jax.numpy as jnp
from jax import lax
from jax.experimental import pallas as pl
from jax.experimental.pallas import tpu as pltpu
from jax.sharding import PartitionSpec as P

LANES = 128
SUBLANES = 8
PIECES = 2
SORTED = 3
EXACT = lax.Precision.HIGHEST
VMEM = pl.BlockSpec(memory_space=pltpu.VMEM)
HBM = pl.BlockSpec(memory_space=pltpu.HBM)
SMEM = pl.BlockSpec(memory_space=pltpu.SMEM)


def iota(shape, dim):
    return lax.broadcasted_iota(jnp.int32, shape, dim)


def band(chunks, rows, cols, shift):
    blocks = []
    for start in range(0, cols, LANES):
        offset = iota((rows, LANES), 1) - iota((rows, LANES), 0) + (shift + start)
        block = None
        turn = jnp.asarray(-(shift + start), jnp.int32) & (LANES - 1)
        for q, chunk in enumerate(chunks):
            first = pltpu.roll(jnp.broadcast_to(chunk, (SUBLANES, LANES)), turn, 1)
            spread = pltpu.roll(
                jnp.broadcast_to(first[:1], (rows, LANES)), 0, 1, stride=1, stride_axis=0
            )
            here = (offset >= q * LANES) & (offset < (q + 1) * LANES)
            part = jnp.where(here, spread, 0.0)
            block = part if block is None else block + part
        blocks.append(block)
    return blocks[0] if len(blocks) == 1 else jnp.concatenate(blocks, axis=1)


def wide(ref, scratch):
    scratch[...] = jnp.zeros_like(scratch)
    scratch[0:1, 0 : ref.shape[1]] = ref[...]
    return scratch[0:1, :]


def dot(a, b):
    return jnp.dot(a, b, precision=EXACT, preferred_element_type=jnp.float32)


def dot_t(a, b):
    return lax.dot_general(
        a, b, (((1,), (1,)), ((), ())), precision=EXACT, preferred_element_type=jnp.float32
    )


def time_kernel(shifts, windows, time_ref, late_ref, x_ref, partial_ref, others_ref, scratch):
    shots, stations, window = x_ref.shape
    half = (time_ref.shape[1] - 1) // 2
    place = lax.axis_index("tm")
    base = window // 2
    late = band([wide(late_ref, scratch)], window, 2 * window, half - base)
    sample = place * window - base + iota((window, 2 * window), 1)
    late = jnp.where((sample >= 0) & (sample < windows * window), late, 0.0)
    taps = wide(time_ref, scratch)
    for n, shift in enumerate((lambda _: 0,) + shifts):
        matrix = dot(late, band([taps], 2 * window, window, shift(place) * window + base + half))
        if n == 0:
            own = dot_t(x_ref[...].reshape(shots * stations, window), matrix)
            partial_ref[...] = own.reshape(partial_ref.shape)
        else:
            others_ref[n - 1] = matrix


def station_kernel(order_ref, rec_ref, live_ref, partial_ref, matrix_ref, *refs):
    *halo_refs, out_ref, scratch, flags, padded, done = refs
    shots, stations, window = partial_ref.shape
    half = (rec_ref.shape[1] - 1) // 2
    flags[0:shots, :] = live_ref[...].astype(jnp.float32)
    columns = jnp.transpose(flags[...])
    edge = LANES // 2
    padded[0:edge, :] = jnp.zeros((edge, shots * window), jnp.float32)
    padded[edge + stations :, :] = jnp.zeros((edge, shots * window), jnp.float32)
    alive = [jnp.broadcast_to(columns[:, s : s + 1], (stations, window)) for s in range(shots)]
    for s in range(shots):
        total = partial_ref[s]
        for n, halo in enumerate(halo_refs):
            total = total + dot_t(halo[s], matrix_ref[n])
        padded[edge : edge + stations, s * window : (s + 1) * window] = total * alive[s]
    matrix = band([wide(rec_ref, scratch)], LANES, 2 * LANES, half - edge)
    for start in range(0, stations, LANES):
        block = dot(matrix, padded[start : start + 2 * LANES, :])
        for s in range(shots):
            done[s, start : start + LANES, :] = (
                block[:, s * window : (s + 1) * window] * alive[s][start : start + LANES]
            )
    groups, _, members, _ = out_ref.shape

    def group(g, carry):
        for q in range(members):
            station = order_ref[g * members + q]
            for s in range(shots):
                out_ref[g, s, pl.ds(q, 1), :] = done[s, pl.ds(station, 1), :]
        return carry

    lax.fori_loop(0, groups, group, 0)


def shot_matrix_kernel(half, taps_ref, out_ref):
    size = out_ref.shape[0]
    chunks = [taps_ref[q : q + 1, :] for q in range(taps_ref.shape[0])]
    out_ref[...] = band(chunks, size, size, SUBLANES * half)


def shot_kernel(matrix_ref, in_ref, out_ref):
    shots, members, window = in_ref.shape
    rows = SUBLANES * shots
    for start in range(0, members, 2 * SUBLANES):
        parts = [
            in_ref[:, a : a + SUBLANES, :].reshape(rows, window)
            for a in (start, start + SUBLANES)
        ]
        result = dot(matrix_ref[...], jnp.concatenate(parts, axis=1))
        for n, a in enumerate((start, start + SUBLANES)):
            out_ref[:, a : a + SUBLANES, :] = result[:, n * window : (n + 1) * window].reshape(
                shots, SUBLANES, window
            )


def split(value, count=2):
    pieces = []
    for _ in range(count):
        pieces.append(value.astype(jnp.bfloat16))
        if len(pieces) < count:
            value = value - pieces[-1].astype(jnp.float32)
    return pieces


def product(a, b):
    terms = ((0, 0), (1, 0), (0, 1))
    return sum(jnp.dot(a[i], b[j], preferred_element_type=jnp.float32) for i, j in terms)


def diagonal(ref, scratch, backwards):
    count = ref.shape[1]
    lane = iota((SUBLANES, LANES), 1) - iota((SUBLANES, LANES), 0)
    used = (lane >= 0) & (lane < count)
    lane = jnp.clip(lane, 0, count - 1)
    taps = jnp.broadcast_to(wide(ref, scratch), (SUBLANES, LANES))
    taps = jnp.take_along_axis(
        taps, count - 1 - lane if backwards else lane, axis=1, mode="promise_in_bounds"
    )
    pieces = split(jnp.where(used, taps, 0.0))
    return [piece.astype(jnp.float32) for piece in pieces], count + SUBLANES - 1


def banded(diagonals, rows, cols, first, mask=None):
    pieces, wide_lanes = diagonals
    lane = iota((SUBLANES, LANES), 1)
    strips = [[] for _ in pieces]
    for row in range(0, rows, SUBLANES):
        start = row + first
        stop = start + wide_lanes
        for n, piece in enumerate(pieces):
            turned = pltpu.roll(piece, start % LANES, 1)
            tiles = []
            for low in range(0, cols, LANES):
                high = low + LANES
                if stop <= low or start >= high:
                    tiles.append(jnp.zeros((SUBLANES, LANES), jnp.float32))
                    continue
                tile = turned
                if start < low:
                    tile = jnp.where(lane < stop - low, tile, 0.0)
                elif stop > high:
                    tile = jnp.where(lane >= start - low, tile, 0.0)
                if mask is not None:
                    tile = tile * mask[:, low:high]
                tiles.append(tile)
            strips[n].append(jnp.concatenate(tiles, axis=1))
    return [jnp.concatenate(parts, axis=0).astype(jnp.bfloat16) for parts in strips]


MARGIN = LANES // 2
REACH = 2 * LANES


def spans(stations):
    step = REACH - 2 * MARGIN
    return [(start, min(step, stations - start)) for start in range(0, stations, step)]


def prepare_kernel(
    time_hbm, late_hbm, rec_hbm, shot_hbm, live_hbm, order_hbm, data_hbm, *refs
):
    times_ref, stations_ref, order_ref, own_ref, across_ref, *refs = refs
    time_ref, late_ref, rec_ref, shot_ref, live_ref, place_ref, data_ref, scratch, flags, sems = refs
    place = lax.axis_index("tm")
    stations, window = data_ref.shape
    samples = 2 * window
    half = (time_ref.shape[1] - 1) // 2
    pairs = (
        (time_hbm, time_ref),
        (late_hbm, late_ref),
        (rec_hbm, rec_ref),
        (shot_hbm, shot_ref),
        (live_hbm, live_ref),
        (order_hbm, place_ref),
        (data_hbm.at[place], data_ref),
    )
    copies = [pltpu.make_async_copy(a, b, sems.at[n]) for n, (a, b) in enumerate(pairs)]
    for copy in copies:
        copy.start()
    flags[...] = jnp.zeros_like(flags)
    for copy in copies[:6]:
        copy.wait()
    time_pieces = banded(diagonal(time_ref, scratch.at[0], True), samples, samples, -half)
    late_pieces = banded(diagonal(late_ref, scratch.at[1], True), samples, samples, -half)
    both = split(product(time_pieces, late_pieces))
    for n, piece in enumerate(both):
        for side in range(2):
            row = pl.multiple_of((place ^ side) * window, window)
            times_ref[n, pl.ds(row, window), :] = piece[side * window : (side + 1) * window, :]
    alive = live_ref[pl.ds(place, 1), :].astype(jnp.float32)
    flags[0:1, MARGIN : MARGIN + stations] = alive
    taps = diagonal(rec_ref, scratch.at[2], False)
    for m, (start, count) in enumerate(spans(stations)):
        mask = jnp.broadcast_to(flags[0:1, start : start + REACH], (SUBLANES, REACH))
        for n, piece in enumerate(banded(taps, count, REACH, MARGIN - half, mask)):
            stations_ref[n, m, 0:count, :] = piece
    order = jnp.broadcast_to(place_ref[...].astype(jnp.float32), (SUBLANES, stations))
    order = jnp.transpose(order)[:, 0:1]
    numbers = iota((stations, stations), 1).astype(jnp.float32)
    order_ref[...] = jnp.where(numbers == order, alive, 0.0).astype(jnp.bfloat16)
    copies[6].wait()
    for n, piece in enumerate(split(data_ref[...])):
        own_ref[n] = piece
    matrix = spread_matrix(shot_ref, scratch.at[3], across_ref.shape[1] // SUBLANES)
    for n, piece in enumerate(matrix):
        across_ref[n] = piece


def sorted_kernel(times_ref, stations_ref, order_ref, own_ref, other_ref, out_ref, *refs):
    padded, done = refs
    place = lax.axis_index("tm")
    _, stations, window = other_ref.shape
    tail = padded.shape[1] - MARGIN - stations
    padded[:, 0:MARGIN, :] = jnp.zeros((PIECES, MARGIN, 2 * window), jnp.bfloat16)
    padded[:, MARGIN + stations :, :] = jnp.zeros((PIECES, tail, 2 * window), jnp.bfloat16)
    other = split(other_ref[place])
    both = [jnp.concatenate([own_ref[n], other[n]], axis=1) for n in range(PIECES)]
    times = [times_ref[n] for n in range(PIECES)]
    step = stations // 2
    for start in range(0, stations, step):
        filtered = product([piece[start : start + step] for piece in both], times)
        for n, piece in enumerate(split(filtered)):
            padded[n, MARGIN + start : MARGIN + start + step, :] = piece
    for m, (start, count) in enumerate(spans(stations)):
        taps = [stations_ref[n, m, 0:count, :] for n in range(PIECES)]
        block = product(taps, [padded[n, start : start + REACH, :] for n in range(PIECES)])
        for n, piece in enumerate(split(block, SORTED)):
            done[n, start : start + count, :] = piece
    groups, _, members, _ = out_ref.shape
    step = groups // 2
    for first in range(0, groups, step):
        pick = order_ref[first * members : (first + step) * members, :]
        rows = sum(
            jnp.dot(pick, done[n], preferred_element_type=jnp.float32)
            for n in reversed(range(SORTED))
        )
        for side in range(2):
            out_ref[first : first + step, side] = rows[
                :, side * window : (side + 1) * window
            ].reshape(step, members, window)


def spread_matrix(ref, scratch, shots):
    count = ref.shape[1]
    half = (count - 1) // 2
    lane = iota((SUBLANES, LANES), 1)
    turn = lane - iota((SUBLANES, LANES), 0)
    taps = jnp.broadcast_to(wide(ref, scratch), (SUBLANES, LANES))
    chunks = []
    for low in range(0, SUBLANES * count, LANES):
        at = turn + low
        used = (at >= 0) & (at < SUBLANES * count) & (at & (SUBLANES - 1) == 0)
        tap = jnp.clip(at >> (SUBLANES.bit_length() - 1), 0, count - 1)
        picked = jnp.take_along_axis(taps, tap, axis=1, mode="promise_in_bounds")
        chunks.append([p.astype(jnp.float32) for p in split(jnp.where(used, picked, 0.0))])
    none = jnp.zeros((SUBLANES, LANES), jnp.float32)
    strips = [[] for _ in range(PIECES)]
    for shot in range(shots):
        start = SUBLANES * (shot - half)
        for n in range(PIECES):
            turned = [pltpu.roll(chunk[n], start % LANES, 1) for chunk in chunks]
            tiles = []
            for low in range(0, SUBLANES * shots, LANES):
                tile = none
                for q in range(len(chunks)):
                    at = start + q * LANES - low
                    if at == 0:
                        tile = turned[q]
                    elif 0 < at < LANES:
                        tile = jnp.where(lane >= at, turned[q], tile)
                    elif -LANES < at < 0:
                        tile = jnp.where(lane < at + LANES, turned[q], tile)
                tiles.append(tile)
            strips[n].append(jnp.concatenate(tiles, axis=1))
    return [jnp.concatenate(parts, axis=0).astype(jnp.bfloat16) for parts in strips]


def across_kernel(matrix_ref, in_ref, out_hbm, result, sems):
    shots, members, window = in_ref.shape
    matrix = [matrix_ref[n] for n in range(PIECES)]
    copies = []
    for start in range(0, members, 2 * SUBLANES):
        parts = [
            in_ref[:, a : a + SUBLANES, :].reshape(SUBLANES * shots, window)
            for a in (start, start + SUBLANES)
        ]
        rows = product(matrix, split(jnp.concatenate(parts, axis=1)))
        for n, a in enumerate((start, start + SUBLANES)):
            result[:, a : a + SUBLANES, :] = rows[:, n * window : (n + 1) * window].reshape(
                shots, SUBLANES, window
            )
        span = (slice(None), pl.ds(start, 2 * SUBLANES))
        copies.append(
            pltpu.make_async_copy(result.at[span], out_hbm.at[span], sems.at[len(copies)])
        )
        copies[-1].start()
    for copy in copies:
        copy.wait()


def still(array):
    return pltpu.with_memory_space_constraint(array, pltpu.HBM)


def paired(shot_data, live_mask, recv_order, rec_taps, time_taps, shot_taps, late_taps):
    shots, stations, window = shot_data.shape
    groups = lax.axis_size("shot")
    members = stations // groups
    f32, bf16 = jnp.float32, jnp.bfloat16
    row = lambda values: values.reshape(1, -1)
    samples = 2 * window
    blocks = spans(stations)
    tap_count = rec_taps.shape[0]
    grant = pltpu.CompilerParams(vmem_limit_bytes=16 * 2**20)
    traded = lax.ppermute(shot_data, "tm", [(0, 1), (1, 0)])
    taps = [row(values) for values in (time_taps, late_taps, rec_taps, shot_taps)]
    total_shots = groups * shots
    spread = SUBLANES * total_shots
    *prepared, matrix = pl.pallas_call(
        prepare_kernel,
        out_shape=[
            jax.ShapeDtypeStruct((PIECES, samples, samples), bf16),
            jax.ShapeDtypeStruct((PIECES, len(blocks), REACH - 2 * MARGIN, REACH), bf16),
            jax.ShapeDtypeStruct((stations, stations), bf16),
            jax.ShapeDtypeStruct((PIECES, stations, window), bf16),
            jax.ShapeDtypeStruct((PIECES, spread, spread), bf16),
        ],
        in_specs=[HBM] * 7,
        out_specs=[VMEM] * 5,
        scratch_shapes=[pltpu.VMEM((1, tap_count), f32)] * 4
        + [
            pltpu.VMEM((shots, stations), jnp.int32),
            pltpu.VMEM((1, stations), jnp.int32),
            pltpu.VMEM((stations, window), f32),
            pltpu.VMEM((4, SUBLANES, LANES), f32),
            pltpu.VMEM((1, blocks[-1][0] + REACH), f32),
            pltpu.SemaphoreType.DMA((7,)),
        ],
        compiler_params=grant,
        cost_estimate=pl.CostEstimate(flops=10**8, bytes_accessed=10**6, transcendentals=0),
    )(*(still(a) for a in (*taps, live_mask, row(recv_order), shot_data)))
    packed = pl.pallas_call(
        sorted_kernel,
        out_shape=jax.ShapeDtypeStruct((groups, 2, members, window), f32),
        in_specs=[VMEM] * 5,
        out_specs=VMEM,
        scratch_shapes=[
            pltpu.VMEM((PIECES, blocks[-1][0] + REACH, samples), bf16),
            pltpu.VMEM((SORTED, stations, samples), bf16),
        ],
        compiler_params=grant,
    )(*prepared, traded)
    packed = packed.reshape(groups * 2, members, window)
    moved = lax.all_to_all(packed, ("shot", "tm"), split_axis=0, concat_axis=0, tiled=True)
    return pl.pallas_call(
        across_kernel,
        out_shape=jax.ShapeDtypeStruct(moved.shape, f32),
        in_specs=[VMEM] * 2,
        out_specs=HBM,
        scratch_shapes=[
            pltpu.VMEM(moved.shape, f32),
            pltpu.SemaphoreType.DMA((members // (2 * SUBLANES),)),
        ],
        compiler_params=grant,
    )(matrix, moved)


def spread_taps(taps):
    spread = lax.pad(taps, jnp.float32(0), [(0, 0, SUBLANES - 1)])
    return jnp.pad(spread, (0, -spread.shape[0] % LANES)).reshape(-1, LANES)


def shards(shot_data, live_mask, recv_order, rec_taps, time_taps, shot_taps, late_taps):
    shots, stations, window = shot_data.shape
    windows = lax.axis_size("tm")
    groups = lax.axis_size("shot")
    if windows == 2 and shots == 2:
        return paired(
            shot_data, live_mask, recv_order, rec_taps, time_taps, shot_taps, late_taps
        )
    f32 = jnp.float32
    up = [(i, i + 1) for i in range(windows - 1)]
    down = [(j, i) for i, j in up]
    halos = [lax.ppermute(shot_data, "tm", up), lax.ppermute(shot_data, "tm", down)]
    shifts = (lambda place: -1, lambda place: 1)
    row = lambda taps: taps.reshape(1, -1)
    partial, matrices = pl.pallas_call(
        functools.partial(time_kernel, shifts, windows),
        out_shape=[
            jax.ShapeDtypeStruct((shots, stations, window), f32),
            jax.ShapeDtypeStruct((len(halos), window, window), f32),
        ],
        compiler_params=pltpu.CompilerParams(vmem_limit_bytes=32 * 2**20),
        in_specs=[VMEM] * 3,
        out_specs=[VMEM] * 2,
        scratch_shapes=[pltpu.VMEM((SUBLANES, LANES), f32)],
        cost_estimate=pl.CostEstimate(flops=10**8, bytes_accessed=10**6, transcendentals=0),
    )(row(time_taps), row(late_taps), shot_data)
    members = stations // groups
    blocks = pl.pallas_call(
        station_kernel,
        out_shape=jax.ShapeDtypeStruct((groups, shots, members, window), f32),
        compiler_params=pltpu.CompilerParams(vmem_limit_bytes=32 * 2**20),
        in_specs=[SMEM] + [VMEM] * (4 + len(halos)),
        out_specs=VMEM,
        scratch_shapes=[
            pltpu.VMEM((SUBLANES, LANES), f32),
            pltpu.VMEM((SUBLANES, stations), f32),
            pltpu.VMEM((stations + LANES, shots * window), f32),
            pltpu.VMEM((shots, stations, window), f32),
        ],
    )(recv_order, row(rec_taps), live_mask, partial, matrices, *halos)
    moved = lax.all_to_all(blocks, "shot", split_axis=0, concat_axis=0, tiled=True)
    total_shots = groups * shots
    moved = moved.reshape(total_shots, members, window)
    matrix = pl.pallas_call(
        functools.partial(shot_matrix_kernel, (shot_taps.shape[0] - 1) // 2),
        out_shape=jax.ShapeDtypeStruct((SUBLANES * total_shots, SUBLANES * total_shots), f32),
        compiler_params=pltpu.CompilerParams(vmem_limit_bytes=32 * 2**20),
        in_specs=[VMEM],
        out_specs=VMEM,
        cost_estimate=pl.CostEstimate(flops=10**6, bytes_accessed=10**6, transcendentals=0),
    )(spread_taps(shot_taps))
    return pl.pallas_call(
        shot_kernel,
        out_shape=jax.ShapeDtypeStruct(moved.shape, f32),
        compiler_params=pltpu.CompilerParams(vmem_limit_bytes=32 * 2**20),
        in_specs=[VMEM] * 2,
        out_specs=VMEM,
    )(matrix, moved)


def solution(mesh):
    placed = (P("shot", None, "tm"), P("shot", None), P(), P(), P(), P(), P())
    return jax.shard_map(
        shards, mesh=mesh, in_specs=placed, out_specs=P(None, "shot", "tm"), check_vma=False
    )
```

time: 88.4 us -> 27.4 us (0.31)
  other arithmetic: 46.2 us -> 0 us
  blocking collectives: 0 us -> 22.6 us
  waiting for transfers between devices: 16.4 us -> 0.1 us
  starting transfers between devices: 14.4 us -> 0.49 us
  local copies, waits for them, and re-layouts: 7.59 us -> 0 us
  Pallas kernels: 0 us -> 4.02 us
  matrix products: 2.65 us -> 0 us
    mul x2 -> x0, other arithmetic: 23.7 us -> none  [the longest x1 23.7 us: shards(): across = slide_filter(first, rec_taps, 1) * alive]
    all_to_all x0 -> x1, blocking collectives: none -> 22.6 us  [paired(): lax.all_to_all(packed, ('shot', 'tm'), split_axis=0, concat_axis=0, tiled...]
    add x1 -> x0, other arithmetic: 21.1 us -> none  [slide_filter(): summed + tap_list[offset] * lax.slice_in_dim(padded, offset, offset + ext...]
    all_to_all x1 -> x0, waiting for transfers between devices: 13.9 us -> none  [shards(): lax.all_to_all(split_rows, 'shot', split_axis=1, concat_axis=0, tiled=True)]
    all_to_all x1 -> x0, starting transfers between devices: 7.82 us -> none  [shards(): lax.all_to_all(split_rows, 'shot', split_axis=1, concat_axis=0, tiled=True)]
    ppermute x4 -> x1, starting transfers between devices: 6.56 us -> 0.49 us  [paired(): traded = lax.ppermute(shot_data, 'tm', [(0, 1), (1, 0)])]
    pallas_call x0 -> x3, Pallas kernels: none -> 4.02 us  [the longest x1 1.64 us: paired(): pl.pallas_call(prepare_kernel, out_shape=[jax.ShapeDtypeStruct((PIECES, s...]
    slice x6 -> x0, local copies, waits for them, and re-layouts: 3.06 us -> none  [the longest x4 2.84 us: slide_filter(): tap_list[offset]]
  transfers between devices with their start and end apart: 5 -> 1, of which waited for: 3 -> 1; matrix products, arithmetic and copies ran while one was open for 4% -> 0% of each run, Pallas kernels for 0% -> 6%
where the time goes in v1:
time: 27.4 us; the launch traced here: 27.3 us
  blocking collectives  22.6 us (82%)
  Pallas kernels  4.02 us (15%)
  starting transfers between devices  0.49 us (2%)
    all_to_all x1, blocking collectives, paired(): lax.all_to_all(packed, ('shot', 'tm'), split_axis=0, concat_axis=0, tiled...  22.6 us
    pallas_call x1, Pallas kernels, paired(): pl.pallas_call(prepare_kernel, out_shape=[jax.ShapeDtypeStruct((PIECES, s...  1.64 us
    pallas_call x1, Pallas kernels, paired(): pl.pallas_call(sorted_kernel, out_shape=jax.ShapeDtypeStruct((groups, 2,...  1.2 us
    pallas_call x1, Pallas kernels, paired(): pl.pallas_call(across_kernel, out_shape=jax.ShapeDtypeStruct(moved.shape,...  1.18 us
  transfers between devices with their start and end apart: 1, of which 1 were waited for; matrix products, arithmetic and copies ran while one was open for 0% of the time, Pallas kernels for 6%

profile of v1, /device:TPU:0, one launch (start us, length us, event | category | flops | bytes accessed | tf_op | source)
XLA Modules:
  0.0 27.3 jit_solution(5922767180213165859)
XLA Ops:
  0.0 0.5 %collective-permute-start = (f32[2,512,128]{2,1,0:T(8,128)}, f32[2,512,128]{2,1,0:T(8,128)S(1)}, u32[]{:S(2)}, u32[]{:S(2)}) collective-permute-start(f32[2,512,128]{2,1,0:T(8,128)} %data_hbm.1), channel_id=1, source_target_pairs={{0,1},{1,0},{2,3},{3,2},{4,5},{5,4},{6,7},{7,6},{8,9},{9,8},{10,11... | collective-permute-start | bytes 1572872 | tf_op jit(solution)/shard_map/ppermute | solution.py:350
  0.5 1.6 %shard_map.73 = (bf16[2,256,256]{2,1,0:T(8,128)(2,1)S(1)}, bf16[2,4,128,256]{3,2,1,0:T(8,128)(2,1)S(1)}, bf16[512,512]{1,0:T(8,128)(2,1)S(1)}, bf16[2,512,128]{2,1,0:T(8,128)(2,1)S(1)}, bf16[2,256,256]{2,1,0:T(8,128)(2,1)S(1)}) custom-call(f32[1,31]{1,0:T(1,128)} %bitcast.8, f32[1,31]{1,0:T(1,128)} %bitcast.9, f32[1,31]{1,0:T(1,128)} %bitcast.10, ...), custom_call_target="tpu_custom_call" | custom-call | flops 100000000 | bytes 1000000 | tf_op jit(solution)/shard_map/pallas_call | solution.py:354
  2.1 0.1 collective-permute-done.other_ref
  2.2 1.2 %shard_map.74 = f32[16,2,32,128]{3,2,1,0:T(8,128)S(1)} custom-call(bf16[2,256,256]{2,1,0:T(8,128)(2,1)S(1)} %get-tuple-element.11.times_ref, bf16[2,4,128,256]{3,2,1,0:T(8,128)(2,1)S(1)} %get-tuple-element.12.stations_ref, bf16[512,512]{1,0:T(8,128)(2,1)S(1)} %get-tuple-element.13.order_ref, bf16[2,512,128]{2,1,0:T(8,128)(2,1)S(1)} %get-tuple-element.14.own_ref, ...), custom_call_target="tpu_custom_call" | custom-call | tf_op jit(solution)/shard_map/pallas_call | solution.py:377
  3.4 22.6 %all_to_all.5.in_ref = f32[32,32,128]{2,1,0:T(8,128)S(1)} all-to-all(f32[32,32,128]{2,1,0:T(8,128)S(1)} %bitcast.6), channel_id=1, replica_groups=mesh['shot'=16,'tm'=2] {'shot','tm'}, dimensions={0} | all-to-all | bytes 1048576 | tf_op jit(solution)/shard_map/all_to_all | solution.py:389
  26.1 1.2 %shard_map.75 = f32[32,32,128]{2,1,0:T(8,128)} custom-call(bf16[2,256,256]{2,1,0:T(8,128)(2,1)S(1)} %get-tuple-element.10.matrix_ref, f32[32,32,128]{2,1,0:T(8,128)S(1)} %all_to_all.5.in_ref), custom_call_target="tpu_custom_call" | custom-call | tf_op jit(solution)/shard_map/pallas_call | solution.py:390
Async XLA Ops:
  0.0 2.2 %collective-permute-start = (f32[2,512,128]{2,1,0:T(8,128)}, f32[2,512,128]{2,1,0:T(8,128)S(1)}, u32[]{:S(2)}, u32[]{:S(2)}) collective-permute-start(f32[2,512,128]{2,1,0:T(8,128)} %data_hbm.1), channel_id=1, source_target_pairs={{0,1},{1,0},{2,3},{3,2},{4,5},{5,4},{6,7},{7,6},{8,9},{9,8},{10,11... | collective-permute-start | bytes 1572872 | tf_op jit(solution)/shard_map/ppermute | solution.py:350

commit v2 on v1

--- a/solution.py
+++ b/solution.py
@@ -9,7 +9,7 @@
 
 LANES = 128
 SUBLANES = 8
-PIECES = 2
+PIECES = 3
 SORTED = 3
 EXACT = lax.Precision.HIGHEST
 VMEM = pl.BlockSpec(memory_space=pltpu.VMEM)
@@ -128,7 +128,7 @@
             )
 
 
-def split(value, count=2):
+def split(value, count=3):
     pieces = []
     for _ in range(count):
         pieces.append(value.astype(jnp.bfloat16))
@@ -138,8 +138,20 @@
 
 
 def product(a, b):
-    terms = ((0, 0), (1, 0), (0, 1))
+    terms = ((0, 0), (1, 0), (2, 0), (0, 1), (1, 1), (0, 2))
     return sum(jnp.dot(a[i], b[j], preferred_element_type=jnp.float32) for i, j in terms)
+
+
+def stacked(a, b):
+    rows = a[0].shape[0]
+    total = None
+    for j in range(PIECES):
+        left = jnp.concatenate(a[: PIECES - j], axis=0) if j < PIECES - 1 else a[0]
+        terms = jnp.dot(left, b[j], preferred_element_type=jnp.float32)
+        for i in range(PIECES - j):
+            term = terms[i * rows : (i + 1) * rows]
+            total = term if total is None else total + term
+    return total
 
 
 def diagonal(ref, scratch, backwards):
@@ -182,12 +194,11 @@
     return [jnp.concatenate(parts, axis=0).astype(jnp.bfloat16) for parts in strips]
 
 
-MARGIN = LANES // 2
-REACH = 2 * LANES
+MARGIN = 16
 
 
 def spans(stations):
-    step = REACH - 2 * MARGIN
+    step = LANES - 2 * MARGIN
     return [(start, min(step, stations - start)) for start in range(0, stations, step)]
 
 
@@ -226,9 +237,11 @@
     flags[0:1, MARGIN : MARGIN + stations] = alive
     taps = diagonal(rec_ref, scratch.at[2], False)
     for m, (start, count) in enumerate(spans(stations)):
-        mask = jnp.broadcast_to(flags[0:1, start : start + REACH], (SUBLANES, REACH))
-        for n, piece in enumerate(banded(taps, count, REACH, MARGIN - half, mask)):
-            stations_ref[n, m, 0:count, :] = piece
+        mask = jnp.broadcast_to(flags[0:1, start : start + LANES], (SUBLANES, LANES))
+        high, middle, low = banded(taps, count, LANES, MARGIN - half, mask)
+        for n, pair in enumerate(((high, high), (middle, middle), (low, high))):
+            for side in range(2):
+                stations_ref[n, m, 0:count, side * LANES : (side + 1) * LANES] = pair[side]
     order = jnp.broadcast_to(place_ref[...].astype(jnp.float32), (SUBLANES, stations))
     order = jnp.transpose(order)[:, 0:1]
     numbers = iota((stations, stations), 1).astype(jnp.float32)
@@ -253,12 +266,18 @@
     times = [times_ref[n] for n in range(PIECES)]
     step = stations // 2
     for start in range(0, stations, step):
-        filtered = product([piece[start : start + step] for piece in both], times)
+        filtered = stacked([piece[start : start + step] for piece in both], times)
         for n, piece in enumerate(split(filtered)):
             padded[n, MARGIN + start : MARGIN + start + step, :] = piece
     for m, (start, count) in enumerate(spans(stations)):
-        taps = [stations_ref[n, m, 0:count, :] for n in range(PIECES)]
-        block = product(taps, [padded[n, start : start + REACH, :] for n in range(PIECES)])
+        high, middle, low = (padded[n, start : start + LANES, :] for n in range(PIECES))
+        near = jnp.concatenate([high, middle], axis=0)
+        far = jnp.concatenate([high, low], axis=0)
+        upper = jnp.concatenate([stations_ref[n, m, 0:count, :] for n in range(2)], axis=0)
+        both = jnp.dot(upper, near, preferred_element_type=jnp.float32)
+        block = both[:count] + both[count:]
+        lower = stations_ref[2, m, 0:count, :]
+        block = block + jnp.dot(lower, far, preferred_element_type=jnp.float32)
         for n, piece in enumerate(split(block, SORTED)):
             done[n, start : start + count, :] = piece
     groups, _, members, _ = out_ref.shape
@@ -355,7 +374,7 @@
         prepare_kernel,
         out_shape=[
             jax.ShapeDtypeStruct((PIECES, samples, samples), bf16),
-            jax.ShapeDtypeStruct((PIECES, len(blocks), REACH - 2 * MARGIN, REACH), bf16),
+            jax.ShapeDtypeStruct((PIECES, len(blocks), LANES - 2 * MARGIN, 2 * LANES), bf16),
             jax.ShapeDtypeStruct((stations, stations), bf16),
             jax.ShapeDtypeStruct((PIECES, stations, window), bf16),
             jax.ShapeDtypeStruct((PIECES, spread, spread), bf16),
@@ -368,7 +387,7 @@
             pltpu.VMEM((1, stations), jnp.int32),
             pltpu.VMEM((stations, window), f32),
             pltpu.VMEM((4, SUBLANES, LANES), f32),
-            pltpu.VMEM((1, blocks[-1][0] + REACH), f32),
+            pltpu.VMEM((1, blocks[-1][0] + LANES), f32),
             pltpu.SemaphoreType.DMA((7,)),
         ],
         compiler_params=grant,
@@ -380,7 +399,7 @@
         in_specs=[VMEM] * 5,
         out_specs=VMEM,
         scratch_shapes=[
-            pltpu.VMEM((PIECES, blocks[-1][0] + REACH, samples), bf16),
+            pltpu.VMEM((PIECES, blocks[-1][0] + LANES, samples), bf16),
             pltpu.VMEM((SORTED, stations, samples), bf16),
         ],
         compiler_params=grant,

time: 27.4 us -> 27.9 us (1.018)
  Pallas kernels: 4.02 us -> 4.56 us
  transfers between devices with their start and end apart: 1 -> 1, of which waited for: 1 -> 0; matrix products, arithmetic and copies ran while one was open for 0% -> 0% of each run, Pallas kernels for 6% -> 6%
where the time goes in v2:
time: 27.9 us; the launch traced here: 27.7 us
  blocking collectives  22.6 us (81%)
  Pallas kernels  4.56 us (16%)
  starting transfers between devices  0.49 us (2%)
    all_to_all x1, blocking collectives, paired(): lax.all_to_all(packed, ('shot', 'tm'), split_axis=0, concat_axis=0, tiled...  22.6 us
    pallas_call x1, Pallas kernels, paired(): pl.pallas_call(prepare_kernel, out_shape=[jax.ShapeDtypeStruct((PIECES, s...  1.74 us
    pallas_call x1, Pallas kernels, paired(): pl.pallas_call(sorted_kernel, out_shape=jax.ShapeDtypeStruct((groups, 2,...  1.44 us
    pallas_call x1, Pallas kernels, paired(): pl.pallas_call(across_kernel, out_shape=jax.ShapeDtypeStruct(moved.shape,...  1.38 us
  transfers between devices with their start and end apart: 1, of which 0 were waited for; matrix products, arithmetic and copies ran while one was open for 0% of the time, Pallas kernels for 6%

profile of v2, /device:TPU:0, one launch (start us, length us, event | category | flops | bytes accessed | tf_op | source)
XLA Modules:
  0.0 27.7 jit_solution(12961040307583930859)
XLA Ops:
  0.0 0.5 %collective-permute-start = (f32[2,512,128]{2,1,0:T(8,128)}, f32[2,512,128]{2,1,0:T(8,128)S(1)}, u32[]{:S(2)}, u32[]{:S(2)}) collective-permute-start(f32[2,512,128]{2,1,0:T(8,128)} %data_hbm.1), channel_id=1, source_target_pairs={{0,1},{1,0},{2,3},{3,2},{4,5},{5,4},{6,7},{7,6},{8,9},{9,8},{10,11... | collective-permute-start | bytes 1572872 | tf_op jit(solution)/shard_map/ppermute | solution.py:369
  0.5 1.7 %shard_map.73 = (bf16[3,256,256]{2,1,0:T(8,128)(2,1)S(1)}, bf16[3,6,96,256]{3,2,1,0:T(8,128)(2,1)S(1)}, bf16[512,512]{1,0:T(8,128)(2,1)S(1)}, bf16[3,512,128]{2,1,0:T(8,128)(2,1)S(1)}, bf16[3,256,256]{2,1,0:T(8,128)(2,1)S(1)}) custom-call(f32[1,31]{1,0:T(1,128)} %bitcast.8, f32[1,31]{1,0:T(1,128)} %bitcast.9, f32[1,31]{1,0:T(1,128)} %bitcast.10, ...), custom_call_target="tpu_custom_call" | custom-call | flops 100000000 | bytes 1000000 | tf_op jit(solution)/shard_map/pallas_call | solution.py:373
  2.2 0.0 collective-permute-done.other_ref
  2.3 1.4 %shard_map.74 = f32[16,2,32,128]{3,2,1,0:T(8,128)S(1)} custom-call(bf16[3,256,256]{2,1,0:T(8,128)(2,1)S(1)} %get-tuple-element.11.times_ref, bf16[3,6,96,256]{3,2,1,0:T(8,128)(2,1)S(1)} %get-tuple-element.12.stations_ref, bf16[512,512]{1,0:T(8,128)(2,1)S(1)} %get-tuple-element.13.order_ref, bf16[3,512,128]{2,1,0:T(8,128)(2,1)S(1)} %get-tuple-element.14.own_ref, ...), custom_call_target="tpu_custom_call" | custom-call | tf_op jit(solution)/shard_map/pallas_call | solution.py:396
  3.7 22.6 %all_to_all.5.in_ref = f32[32,32,128]{2,1,0:T(8,128)S(1)} all-to-all(f32[32,32,128]{2,1,0:T(8,128)S(1)} %bitcast.6), channel_id=1, replica_groups=mesh['shot'=16,'tm'=2] {'shot','tm'}, dimensions={0} | all-to-all | bytes 1048576 | tf_op jit(solution)/shard_map/all_to_all | solution.py:408
  26.3 1.4 %shard_map.75 = f32[32,32,128]{2,1,0:T(8,128)} custom-call(bf16[3,256,256]{2,1,0:T(8,128)(2,1)S(1)} %get-tuple-element.10.matrix_ref, f32[32,32,128]{2,1,0:T(8,128)S(1)} %all_to_all.5.in_ref), custom_call_target="tpu_custom_call" | custom-call | tf_op jit(solution)/shard_map/pallas_call | solution.py:409
Async XLA Ops:
  0.0 2.2 %collective-permute-start = (f32[2,512,128]{2,1,0:T(8,128)}, f32[2,512,128]{2,1,0:T(8,128)S(1)}, u32[]{:S(2)}, u32[]{:S(2)}) collective-permute-start(f32[2,512,128]{2,1,0:T(8,128)} %data_hbm.1), channel_id=1, source_target_pairs={{0,1},{1,0},{2,3},{3,2},{4,5},{5,4},{6,7},{7,6},{8,9},{9,8},{10,11... | collective-permute-start | bytes 1572872 | tf_op jit(solution)/shard_map/ppermute | solution.py:369

commit v3 on v2

--- a/solution.py
+++ b/solution.py
@@ -194,6 +194,20 @@
     return [jnp.concatenate(parts, axis=0).astype(jnp.bfloat16) for parts in strips]
 
 
+def doubled(a):
+    near = jnp.concatenate([a[0], a[1]], axis=1)
+    return near, near, jnp.concatenate([a[2], a[0]], axis=1)
+
+
+def piled(b):
+    pairs = ((b[0], b[0]), (b[1], b[1]), (b[0], b[2]))
+    return [jnp.concatenate(pair, axis=0) for pair in pairs]
+
+
+def packed_product(a, b):
+    return sum(jnp.dot(x, y, preferred_element_type=jnp.float32) for x, y in zip(a, b))
+
+
 MARGIN = 16
 
 
@@ -206,6 +220,7 @@
     time_hbm, late_hbm, rec_hbm, shot_hbm, live_hbm, order_hbm, data_hbm, *refs
 ):
     times_ref, stations_ref, order_ref, own_ref, across_ref, *refs = refs
+    *refs, matrix_ref = refs
     time_ref, late_ref, rec_ref, shot_ref, live_ref, place_ref, data_ref, scratch, flags, sems = refs
     place = lax.axis_index("tm")
     stations, window = data_ref.shape
@@ -228,11 +243,20 @@
         copy.wait()
     time_pieces = banded(diagonal(time_ref, scratch.at[0], True), samples, samples, -half)
     late_pieces = banded(diagonal(late_ref, scratch.at[1], True), samples, samples, -half)
-    both = split(product(time_pieces, late_pieces))
-    for n, piece in enumerate(both):
-        for side in range(2):
-            row = pl.multiple_of((place ^ side) * window, window)
-            times_ref[n, pl.ds(row, window), :] = piece[side * window : (side + 1) * window, :]
+    for side in range(2):
+        rows = slice(side * window, (side + 1) * window)
+        combined = product([piece[rows] for piece in time_pieces], late_pieces)
+        for n, piece in enumerate(split(combined)):
+            matrix_ref[n, rows, :] = piece
+    copies[6].wait()
+    sides = [pl.ds(pl.multiple_of((place ^ side) * window, window), window) for side in range(2)]
+    own, other = (piled([matrix_ref[n, side, :] for n in range(PIECES)]) for side in sides)
+    for n, piece in enumerate(other):
+        times_ref[n] = piece
+    halves = [slice(start, start + stations // 2) for start in (0, stations // 2)]
+    lefts = [doubled(split(data_ref[rows, :])) for rows in halves]
+    for rows, left in zip(halves, lefts):
+        own_ref[rows, :] = packed_product(left, own)
     alive = live_ref[pl.ds(place, 1), :].astype(jnp.float32)
     flags[0:1, MARGIN : MARGIN + stations] = alive
     taps = diagonal(rec_ref, scratch.at[2], False)
@@ -246,9 +270,6 @@
     order = jnp.transpose(order)[:, 0:1]
     numbers = iota((stations, stations), 1).astype(jnp.float32)
     order_ref[...] = jnp.where(numbers == order, alive, 0.0).astype(jnp.bfloat16)
-    copies[6].wait()
-    for n, piece in enumerate(split(data_ref[...])):
-        own_ref[n] = piece
     matrix = spread_matrix(shot_ref, scratch.at[3], across_ref.shape[1] // SUBLANES)
     for n, piece in enumerate(matrix):
         across_ref[n] = piece
@@ -261,12 +282,12 @@
     tail = padded.shape[1] - MARGIN - stations
     padded[:, 0:MARGIN, :] = jnp.zeros((PIECES, MARGIN, 2 * window), jnp.bfloat16)
     padded[:, MARGIN + stations :, :] = jnp.zeros((PIECES, tail, 2 * window), jnp.bfloat16)
-    other = split(other_ref[place])
-    both = [jnp.concatenate([own_ref[n], other[n]], axis=1) for n in range(PIECES)]
     times = [times_ref[n] for n in range(PIECES)]
     step = stations // 2
     for start in range(0, stations, step):
-        filtered = stacked([piece[start : start + step] for piece in both], times)
+        rows = slice(start, start + step)
+        left = doubled(split(other_ref[place, rows, :]))
+        filtered = own_ref[rows, :] + packed_product(left, times)
         for n, piece in enumerate(split(filtered)):
             padded[n, MARGIN + start : MARGIN + start + step, :] = piece
     for m, (start, count) in enumerate(spans(stations)):
@@ -338,16 +359,20 @@
             in_ref[:, a : a + SUBLANES, :].reshape(SUBLANES * shots, window)
             for a in (start, start + SUBLANES)
         ]
-        rows = product(matrix, split(jnp.concatenate(parts, axis=1)))
-        for n, a in enumerate((start, start + SUBLANES)):
-            result[:, a : a + SUBLANES, :] = rows[:, n * window : (n + 1) * window].reshape(
-                shots, SUBLANES, window
+        inputs = split(jnp.concatenate(parts, axis=1))
+        step = shots // 2
+        for first in range(0, shots, step):
+            lines = slice(SUBLANES * first, SUBLANES * (first + step))
+            rows = product([piece[lines] for piece in matrix], inputs)
+            for n, a in enumerate((start, start + SUBLANES)):
+                result[first : first + step, a : a + SUBLANES, :] = rows[
+                    :, n * window : (n + 1) * window
+                ].reshape(step, SUBLANES, window)
+            span = (pl.ds(first, step), pl.ds(start, 2 * SUBLANES))
+            copies.append(
+                pltpu.make_async_copy(result.at[span], out_hbm.at[span], sems.at[len(copies)])
             )
-        span = (slice(None), pl.ds(start, 2 * SUBLANES))
-        copies.append(
-            pltpu.make_async_copy(result.at[span], out_hbm.at[span], sems.at[len(copies)])
-        )
-        copies[-1].start()
+            copies[-1].start()
     for copy in copies:
         copy.wait()
 
@@ -376,7 +401,7 @@
             jax.ShapeDtypeStruct((PIECES, samples, samples), bf16),
             jax.ShapeDtypeStruct((PIECES, len(blocks), LANES - 2 * MARGIN, 2 * LANES), bf16),
             jax.ShapeDtypeStruct((stations, stations), bf16),
-            jax.ShapeDtypeStruct((PIECES, stations, window), bf16),
+            jax.ShapeDtypeStruct((stations, samples), f32),
             jax.ShapeDtypeStruct((PIECES, spread, spread), bf16),
         ],
         in_specs=[HBM] * 7,
@@ -389,6 +414,7 @@
             pltpu.VMEM((4, SUBLANES, LANES), f32),
             pltpu.VMEM((1, blocks[-1][0] + LANES), f32),
             pltpu.SemaphoreType.DMA((7,)),
+            pltpu.VMEM((PIECES, samples, samples), bf16),
         ],
         compiler_params=grant,
         cost_estimate=pl.CostEstimate(flops=10**8, bytes_accessed=10**6, transcendentals=0),
@@ -413,7 +439,7 @@
         out_specs=HBM,
         scratch_shapes=[
             pltpu.VMEM(moved.shape, f32),
-            pltpu.SemaphoreType.DMA((members // (2 * SUBLANES),)),
+            pltpu.SemaphoreType.DMA((2 * members // (2 * SUBLANES),)),
         ],
         compiler_params=grant,
     )(matrix, moved)

time: 27.9 us -> 27.7 us (level)
  transfers between devices with their start and end apart: 1 -> 1, of which waited for: 0 -> 0; matrix products, arithmetic and copies ran while one was open for 0% -> 0% of each run, Pallas kernels for 6% -> 7%
where the time goes in v3:
time: 27.7 us; the launch traced here: 27.5 us
  blocking collectives  22.4 us (81%)
  Pallas kernels  4.61 us (17%)
  starting transfers between devices  0.49 us (2%)
    all_to_all x1, blocking collectives, paired(): lax.all_to_all(packed, ('shot', 'tm'), split_axis=0, concat_axis=0, tiled...  22.4 us
    pallas_call x1, Pallas kernels, paired(): pl.pallas_call(prepare_kernel, out_shape=[jax.ShapeDtypeStruct((PIECES, s...  2.02 us
    pallas_call x1, Pallas kernels, paired(): pl.pallas_call(across_kernel, out_shape=jax.ShapeDtypeStruct(moved.shape,...  1.33 us
    pallas_call x1, Pallas kernels, paired(): pl.pallas_call(sorted_kernel, out_shape=jax.ShapeDtypeStruct((groups, 2,...  1.26 us
  transfers between devices with their start and end apart: 1, of which 0 were waited for; matrix products, arithmetic and copies ran while one was open for 0% of the time, Pallas kernels for 7%

profile of v3, /device:TPU:0, one launch (start us, length us, event | category | flops | bytes accessed | tf_op | source)
XLA Modules:
  0.0 27.5 jit_solution(17390069902001253120)
XLA Ops:
  0.0 0.5 %collective-permute-start = (f32[2,512,128]{2,1,0:T(8,128)}, f32[2,512,128]{2,1,0:T(8,128)S(1)}, u32[]{:S(2)}, u32[]{:S(2)}) collective-permute-start(f32[2,512,128]{2,1,0:T(8,128)} %data_hbm.1), channel_id=1, source_target_pairs={{0,1},{1,0},{2,3},{3,2},{4,5},{5,4},{6,7},{7,6},{8,9},{9,8},{10,11... | collective-permute-start | bytes 1572872 | tf_op jit(solution)/shard_map/ppermute | solution.py:394
  0.5 2.0 %shard_map.73 = (bf16[3,256,256]{2,1,0:T(8,128)(2,1)S(1)}, bf16[3,6,96,256]{3,2,1,0:T(8,128)(2,1)S(1)}, bf16[512,512]{1,0:T(8,128)(2,1)S(1)}, f32[512,256]{1,0:T(8,128)S(1)}, bf16[3,256,256]{2,1,0:T(8,128)(2,1)S(1)}) custom-call(f32[1,31]{1,0:T(1,128)} %bitcast.8, f32[1,31]{1,0:T(1,128)} %bitcast.9, f32[1,31]{1,0:T(1,128)} %bitcast.10, f32[1,31]{1,0:T(1,128)} %bitcast.11, ...), custom_call_target="tpu_custom_call" | custom-call | flops 100000000 | bytes 1000000 | tf_op jit(solution)/shard_map/pallas_call | solution.py:398
  2.5 0.0 collective-permute-done.other_ref
  2.5 1.3 %shard_map.74 = f32[16,2,32,128]{3,2,1,0:T(8,128)S(1)} custom-call(bf16[3,256,256]{2,1,0:T(8,128)(2,1)S(1)} %get-tuple-element.11.times_ref, bf16[3,6,96,256]{3,2,1,0:T(8,128)(2,1)S(1)} %get-tuple-element.12.stations_ref, bf16[512,512]{1,0:T(8,128)(2,1)S(1)} %get-tuple-element.13.order_ref, f32[512,256]{1,0:T(8,128)S(1)} %get-tuple-element.14.own_ref, ...), custom_call_target="tpu_custom_call" | custom-call | tf_op jit(solution)/shard_map/pallas_call | solution.py:422
  3.8 22.4 %all_to_all.5.in_ref = f32[32,32,128]{2,1,0:T(8,128)S(1)} all-to-all(f32[32,32,128]{2,1,0:T(8,128)S(1)} %bitcast.6), channel_id=1, replica_groups=mesh['shot'=16,'tm'=2] {'shot','tm'}, dimensions={0} | all-to-all | bytes 1048576 | tf_op jit(solution)/shard_map/all_to_all | solution.py:434
  26.2 1.3 %shard_map.75 = f32[32,32,128]{2,1,0:T(8,128)} custom-call(bf16[3,256,256]{2,1,0:T(8,128)(2,1)S(1)} %get-tuple-element.10.matrix_ref, f32[32,32,128]{2,1,0:T(8,128)S(1)} %all_to_all.5.in_ref), custom_call_target="tpu_custom_call" | custom-call | tf_op jit(solution)/shard_map/pallas_call | solution.py:435
Async XLA Ops:
  0.0 2.5 %collective-permute-start = (f32[2,512,128]{2,1,0:T(8,128)}, f32[2,512,128]{2,1,0:T(8,128)S(1)}, u32[]{:S(2)}, u32[]{:S(2)}) collective-permute-start(f32[2,512,128]{2,1,0:T(8,128)} %data_hbm.1), channel_id=1, source_target_pairs={{0,1},{1,0},{2,3},{3,2},{4,5},{5,4},{6,7},{7,6},{8,9},{9,8},{10,11... | collective-permute-start | bytes 1572872 | tf_op jit(solution)/shard_map/ppermute | solution.py:394

commit v4 on v3

--- a/solution.py
+++ b/solution.py
@@ -1,4 +1,5 @@
 import functools
+import math
 
 import jax
 import jax.numpy as jnp
@@ -275,7 +276,7 @@
         across_ref[n] = piece
 
 
-def sorted_kernel(times_ref, stations_ref, order_ref, own_ref, other_ref, out_ref, *refs):
+def sorted_kernel(slots, times_ref, stations_ref, order_ref, own_ref, other_ref, out_ref, *refs):
     padded, done = refs
     place = lax.axis_index("tm")
     _, stations, window = other_ref.shape
@@ -301,7 +302,8 @@
         block = block + jnp.dot(lower, far, preferred_element_type=jnp.float32)
         for n, piece in enumerate(split(block, SORTED)):
             done[n, start : start + count, :] = piece
-    groups, _, members, _ = out_ref.shape
+    devices, members, _ = out_ref.shape
+    groups = devices // 2
     step = groups // 2
     for first in range(0, groups, step):
         pick = order_ref[first * members : (first + step) * members, :]
@@ -309,10 +311,11 @@
             jnp.dot(pick, done[n], preferred_element_type=jnp.float32)
             for n in reversed(range(SORTED))
         )
-        for side in range(2):
-            out_ref[first : first + step, side] = rows[
-                :, side * window : (side + 1) * window
-            ].reshape(step, members, window)
+        for group in range(step):
+            lines = slice(group * members, (group + 1) * members)
+            for side in range(2):
+                part = rows[lines, side * window : (side + 1) * window]
+                out_ref[slots[2 * (first + group) + side]] = part
 
 
 def spread_matrix(ref, scratch, shots):
@@ -350,13 +353,13 @@
     return [jnp.concatenate(parts, axis=0).astype(jnp.bfloat16) for parts in strips]
 
 
-def across_kernel(matrix_ref, in_ref, out_hbm, result, sems):
+def across_kernel(slots, matrix_ref, in_ref, out_hbm, result, sems):
     shots, members, window = in_ref.shape
     matrix = [matrix_ref[n] for n in range(PIECES)]
     copies = []
     for start in range(0, members, 2 * SUBLANES):
         parts = [
-            in_ref[:, a : a + SUBLANES, :].reshape(SUBLANES * shots, window)
+            jnp.concatenate([in_ref[slot, a : a + SUBLANES, :] for slot in slots], axis=0)
             for a in (start, start + SUBLANES)
         ]
         inputs = split(jnp.concatenate(parts, axis=1))
@@ -381,6 +384,14 @@
     return pltpu.with_memory_space_constraint(array, pltpu.HBM)
 
 
+STRIDE = 7
+
+
+def visiting_order(count):
+    stride = STRIDE if math.gcd(STRIDE, count) == 1 else 1
+    return [(n * stride) % count for n in range(count)]
+
+
 def paired(shot_data, live_mask, recv_order, rec_taps, time_taps, shot_taps, late_taps):
     shots, stations, window = shot_data.shape
     groups = lax.axis_size("shot")
@@ -394,6 +405,8 @@
     traded = lax.ppermute(shot_data, "tm", [(0, 1), (1, 0)])
     taps = [row(values) for values in (time_taps, late_taps, rec_taps, shot_taps)]
     total_shots = groups * shots
+    order = visiting_order(2 * groups)
+    slots = [order.index(device) for device in range(2 * groups)]
     spread = SUBLANES * total_shots
     *prepared, matrix = pl.pallas_call(
         prepare_kernel,
@@ -420,8 +433,8 @@
         cost_estimate=pl.CostEstimate(flops=10**8, bytes_accessed=10**6, transcendentals=0),
     )(*(still(a) for a in (*taps, live_mask, row(recv_order), shot_data)))
     packed = pl.pallas_call(
-        sorted_kernel,
-        out_shape=jax.ShapeDtypeStruct((groups, 2, members, window), f32),
+        functools.partial(sorted_kernel, slots),
+        out_shape=jax.ShapeDtypeStruct((2 * groups, members, window), f32),
         in_specs=[VMEM] * 5,
         out_specs=VMEM,
         scratch_shapes=[
@@ -430,10 +443,16 @@
         ],
         compiler_params=grant,
     )(*prepared, traded)
-    packed = packed.reshape(groups * 2, members, window)
-    moved = lax.all_to_all(packed, ("shot", "tm"), split_axis=0, concat_axis=0, tiled=True)
+    moved = lax.all_to_all(
+        packed,
+        ("shot", "tm"),
+        split_axis=0,
+        concat_axis=0,
+        tiled=True,
+        axis_index_groups=[order],
+    )
     return pl.pallas_call(
-        across_kernel,
+        functools.partial(across_kernel, slots),
         out_shape=jax.ShapeDtypeStruct(moved.shape, f32),
         in_specs=[VMEM] * 2,
         out_specs=HBM,

time: 27.7 us -> 27 us (0.975)
  blocking collectives: 22.4 us -> 21.7 us
    all_to_all x1, blocking collectives: 22.4 us -> 21.7 us  [paired(): lax.all_to_all(packed, ('shot', 'tm'), split_axis=0, concat_axis=0, tiled...]
  transfers between devices with their start and end apart: 1 -> 1, of which waited for: 0 -> 0; matrix products, arithmetic and copies ran while one was open for 0% -> 0% of each run, Pallas kernels for 7% -> 8%
where the time goes in v4:
time: 27 us; the launch traced here: 26.9 us
  blocking collectives  21.7 us (80%)
  Pallas kernels  4.61 us (17%)
  starting transfers between devices  0.49 us (2%)
    all_to_all x1, blocking collectives, paired(): lax.all_to_all(packed, ('shot', 'tm'), split_axis=0, concat_axis=0, tiled...  21.7 us
    pallas_call x1, Pallas kernels, paired(): pl.pallas_call(prepare_kernel, out_shape=[jax.ShapeDtypeStruct((PIECES, s...  2.02 us
    pallas_call x1, Pallas kernels, paired(): pl.pallas_call(functools.partial(across_kernel, slots), out_shape=jax.Sha...  1.34 us
    pallas_call x1, Pallas kernels, paired(): pl.pallas_call(functools.partial(sorted_kernel, slots), out_shape=jax.Sha...  1.26 us
  transfers between devices with their start and end apart: 1, of which 0 were waited for; matrix products, arithmetic and copies ran while one was open for 0% of the time, Pallas kernels for 8%

profile of v4, /device:TPU:0, one launch (start us, length us, event | category | flops | bytes accessed | tf_op | source)
XLA Modules:
  0.0 26.9 jit_solution(17977472243919580889)
XLA Ops:
  0.0 0.5 %collective-permute-start = (f32[2,512,128]{2,1,0:T(8,128)}, f32[2,512,128]{2,1,0:T(8,128)S(1)}, u32[]{:S(2)}, u32[]{:S(2)}) collective-permute-start(f32[2,512,128]{2,1,0:T(8,128)} %data_hbm.1), channel_id=1, source_target_pairs={{0,1},{1,0},{2,3},{3,2},{4,5},{5,4},{6,7},{7,6},{8,9},{9,8},{10,11... | collective-permute-start | bytes 1572872 | tf_op jit(solution)/shard_map/ppermute | solution.py:405
  0.5 2.0 %shard_map.73 = (bf16[3,256,256]{2,1,0:T(8,128)(2,1)S(1)}, bf16[3,6,96,256]{3,2,1,0:T(8,128)(2,1)S(1)}, bf16[512,512]{1,0:T(8,128)(2,1)S(1)}, f32[512,256]{1,0:T(8,128)S(1)}, bf16[3,256,256]{2,1,0:T(8,128)(2,1)S(1)}) custom-call(f32[1,31]{1,0:T(1,128)} %bitcast.6, f32[1,31]{1,0:T(1,128)} %bitcast.7, f32[1,31]{1,0:T(1,128)} %bitcast.8, f32[1,31]{1,0:T(1,128)} %bitcast.9, ...), custom_call_target="tpu_custom_call" | custom-call | flops 100000000 | bytes 1000000 | tf_op jit(solution)/shard_map/pallas_call | solution.py:411
  2.5 0.0 collective-permute-done.other_ref
  2.5 1.3 %shard_map.74 = f32[32,32,128]{2,1,0:T(8,128)S(1)} custom-call(bf16[3,256,256]{2,1,0:T(8,128)(2,1)S(1)} %get-tuple-element.11.times_ref, bf16[3,6,96,256]{3,2,1,0:T(8,128)(2,1)S(1)} %get-tuple-element.12.stations_ref, bf16[512,512]{1,0:T(8,128)(2,1)S(1)} %get-tuple-element.13.order_ref, f32[512,256]{1,0:T(8,128)S(1)} %get-tuple-element.14.own_ref, ...), custom_call_target="tpu_custom_call" | custom-call | tf_op jit(solution)/shard_map/pallas_call | solution.py:435
  3.8 21.7 %all_to_all.5.in_ref = f32[32,32,128]{2,1,0:T(8,128)S(1)} all-to-all(f32[32,32,128]{2,1,0:T(8,128)S(1)} %shard_map.74), channel_id=1, replica_groups={{0,7,14,21,28,3,10,17,24,31,6,13,20,27,2,9,16,23,30,5,12,19,26,1,8,15,2..., dimensions={0} | all-to-all | bytes 1048576 | tf_op jit(solution)/shard_map/all_to_all | solution.py:446
  25.5 1.3 %shard_map.75 = f32[32,32,128]{2,1,0:T(8,128)} custom-call(bf16[3,256,256]{2,1,0:T(8,128)(2,1)S(1)} %get-tuple-element.10.matrix_ref, f32[32,32,128]{2,1,0:T(8,128)S(1)} %all_to_all.5.in_ref), custom_call_target="tpu_custom_call" | custom-call | tf_op jit(solution)/shard_map/pallas_call | solution.py:454
Async XLA Ops:
  0.0 2.5 %collective-permute-start = (f32[2,512,128]{2,1,0:T(8,128)}, f32[2,512,128]{2,1,0:T(8,128)S(1)}, u32[]{:S(2)}, u32[]{:S(2)}) collective-permute-start(f32[2,512,128]{2,1,0:T(8,128)} %data_hbm.1), channel_id=1, source_target_pairs={{0,1},{1,0},{2,3},{3,2},{4,5},{5,4},{6,7},{7,6},{8,9},{9,8},{10,11... | collective-permute-start | bytes 1572872 | tf_op jit(solution)/shard_map/ppermute | solution.py:405

commit v5 on v4

--- a/solution.py
+++ b/solution.py
@@ -220,7 +220,7 @@
 def prepare_kernel(
     time_hbm, late_hbm, rec_hbm, shot_hbm, live_hbm, order_hbm, data_hbm, *refs
 ):
-    times_ref, stations_ref, order_ref, own_ref, across_ref, *refs = refs
+    times_ref, stations_ref, order_ref, alive_ref, own_ref, across_ref, *refs = refs
     *refs, matrix_ref = refs
     time_ref, late_ref, rec_ref, shot_ref, live_ref, place_ref, data_ref, scratch, flags, sems = refs
     place = lax.axis_index("tm")
@@ -268,15 +268,23 @@
             for side in range(2):
                 stations_ref[n, m, 0:count, side * LANES : (side + 1) * LANES] = pair[side]
     order = jnp.broadcast_to(place_ref[...].astype(jnp.float32), (SUBLANES, stations))
-    order = jnp.transpose(order)[:, 0:1]
-    numbers = iota((stations, stations), 1).astype(jnp.float32)
-    order_ref[...] = jnp.where(numbers == order, alive, 0.0).astype(jnp.bfloat16)
+    order_ref[...] = jnp.broadcast_to(jnp.transpose(order)[:, 0:1], order_ref.shape)
+    alive_ref[...] = jnp.broadcast_to(alive, alive_ref.shape)
     matrix = spread_matrix(shot_ref, scratch.at[3], across_ref.shape[1] // SUBLANES)
     for n, piece in enumerate(matrix):
         across_ref[n] = piece
 
 
-def sorted_kernel(slots, times_ref, stations_ref, order_ref, own_ref, other_ref, out_ref, *refs):
+def chosen(order, alive):
+    lane = iota(order.shape, 1).astype(jnp.float32)
+    tiles = [
+        jnp.where(order == lane + float(low), alive[0:1, low : low + LANES], 0.0)
+        for low in range(0, alive.shape[1], LANES)
+    ]
+    return jnp.concatenate(tiles, axis=1).astype(jnp.bfloat16)
+
+
+def sorted_kernel(slots, times_ref, stations_ref, order_ref, alive_ref, own_ref, other_ref, out_ref, *refs):
     padded, done = refs
     place = lax.axis_index("tm")
     _, stations, window = other_ref.shape
@@ -285,6 +293,10 @@
     padded[:, MARGIN + stations :, :] = jnp.zeros((PIECES, tail, 2 * window), jnp.bfloat16)
     times = [times_ref[n] for n in range(PIECES)]
     step = stations // 2
+    picks = [
+        chosen(order_ref[start : start + step, :], alive_ref[...])
+        for start in range(0, stations, step)
+    ]
     for start in range(0, stations, step):
         rows = slice(start, start + step)
         left = doubled(split(other_ref[place, rows, :]))
@@ -306,7 +318,7 @@
     groups = devices // 2
     step = groups // 2
     for first in range(0, groups, step):
-        pick = order_ref[first * members : (first + step) * members, :]
+        pick = picks[first // step]
         rows = sum(
             jnp.dot(pick, done[n], preferred_element_type=jnp.float32)
             for n in reversed(range(SORTED))
@@ -413,12 +425,13 @@
         out_shape=[
             jax.ShapeDtypeStruct((PIECES, samples, samples), bf16),
             jax.ShapeDtypeStruct((PIECES, len(blocks), LANES - 2 * MARGIN, 2 * LANES), bf16),
-            jax.ShapeDtypeStruct((stations, stations), bf16),
+            jax.ShapeDtypeStruct((stations, LANES), f32),
+            jax.ShapeDtypeStruct((SUBLANES, stations), f32),
             jax.ShapeDtypeStruct((stations, samples), f32),
             jax.ShapeDtypeStruct((PIECES, spread, spread), bf16),
         ],
         in_specs=[HBM] * 7,
-        out_specs=[VMEM] * 5,
+        out_specs=[VMEM] * 6,
         scratch_shapes=[pltpu.VMEM((1, tap_count), f32)] * 4
         + [
             pltpu.VMEM((shots, stations), jnp.int32),
@@ -435,7 +448,7 @@
     packed = pl.pallas_call(
         functools.partial(sorted_kernel, slots),
         out_shape=jax.ShapeDtypeStruct((2 * groups, members, window), f32),
-        in_specs=[VMEM] * 5,
+        in_specs=[VMEM] * 6,
         out_specs=VMEM,
         scratch_shapes=[
             pltpu.VMEM((PIECES, blocks[-1][0] + LANES, samples), bf16),

time: 27 us -> 27 us (level)
  transfers between devices with their start and end apart: 1 -> 1, of which waited for: 0 -> 0; matrix products, arithmetic and copies ran while one was open for 0% -> 0% of each run, Pallas kernels for 8% -> 7%
where the time goes in v5:
time: 27 us; the launch traced here: 26.8 us
  blocking collectives  21.8 us (81%)
  Pallas kernels  4.56 us (17%)
  starting transfers between devices  0.49 us (2%)
    all_to_all x1, blocking collectives, paired(): lax.all_to_all(packed, ('shot', 'tm'), split_axis=0, concat_axis=0, tiled...  21.8 us
    pallas_call x1, Pallas kernels, paired(): pl.pallas_call(prepare_kernel, out_shape=[jax.ShapeDtypeStruct((PIECES, s...  1.97 us
    pallas_call x1, Pallas kernels, paired(): pl.pallas_call(functools.partial(across_kernel, slots), out_shape=jax.Sha...  1.34 us
    pallas_call x1, Pallas kernels, paired(): pl.pallas_call(functools.partial(sorted_kernel, slots), out_shape=jax.Sha...  1.25 us
  transfers between devices with their start and end apart: 1, of which 0 were waited for; matrix products, arithmetic and copies ran while one was open for 0% of the time, Pallas kernels for 7%

profile of v5, /device:TPU:0, one launch (start us, length us, event | category | flops | bytes accessed | tf_op | source)
XLA Modules:
  0.0 26.8 jit_solution(14197620094005587193)
XLA Ops:
  0.0 0.5 %collective-permute-start = (f32[2,512,128]{2,1,0:T(8,128)}, f32[2,512,128]{2,1,0:T(8,128)S(1)}, u32[]{:S(2)}, u32[]{:S(2)}) collective-permute-start(f32[2,512,128]{2,1,0:T(8,128)} %data_hbm.1), channel_id=1, source_target_pairs={{0,1},{1,0},{2,3},{3,2},{4,5},{5,4},{6,7},{7,6},{8,9},{9,8},{10,11... | collective-permute-start | bytes 1572872 | tf_op jit(solution)/shard_map/ppermute | solution.py:417
  0.5 2.0 %shard_map.73 = (bf16[3,256,256]{2,1,0:T(8,128)(2,1)S(1)}, bf16[3,6,96,256]{3,2,1,0:T(8,128)(2,1)S(1)}, f32[512,128]{1,0:T(8,128)S(1)}, f32[8,512]{1,0:T(8,128)S...) custom-call(f32[1,31]{1,0:T(1,128)} %bitcast.6, f32[1,31]{1,0:T(1,128)} %bitcast.7, f32[1,31]{1,0:T(1,128)} %bitcast.8, ...), custom_call_target="tpu_custom_call" | custom-call | flops 100000000 | bytes 1000000 | tf_op jit(solution)/shard_map/pallas_call | solution.py:423
  2.5 0.0 collective-permute-done.other_ref
  2.5 1.3 %shard_map.74 = f32[32,32,128]{2,1,0:T(8,128)S(1)} custom-call(bf16[3,256,256]{2,1,0:T(8,128)(2,1)S(1)} %get-tuple-element.12.times_ref, bf16[3,6,96,256]{3,2,1,0:T(8,128)(2,1)S(1)} %get-tuple-element.13.stations_ref, f32[512,128]{1,0:T(8,128)S(1)} %get-tuple-element.14.order_ref, f32[8,512]{1,0:T(8,128)S(1)} %get-tuple-element.15.alive_ref, ...), custom_call_target="tpu_custom_call" | custom-call | tf_op jit(solution)/shard_map/pallas_call | solution.py:448
  3.7 21.8 %all_to_all.5.in_ref = f32[32,32,128]{2,1,0:T(8,128)S(1)} all-to-all(f32[32,32,128]{2,1,0:T(8,128)S(1)} %shard_map.74), channel_id=1, replica_groups={{0,7,14,21,28,3,10,17,24,31,6,13,20,27,2,9,16,23,30,5,12,19,26,1,8,15,2..., dimensions={0} | all-to-all | bytes 1048576 | tf_op jit(solution)/shard_map/all_to_all | solution.py:459
  25.5 1.3 %shard_map.75 = f32[32,32,128]{2,1,0:T(8,128)} custom-call(bf16[3,256,256]{2,1,0:T(8,128)(2,1)S(1)} %get-tuple-element.11.matrix_ref, f32[32,32,128]{2,1,0:T(8,128)S(1)} %all_to_all.5.in_ref), custom_call_target="tpu_custom_call" | custom-call | tf_op jit(solution)/shard_map/pallas_call | solution.py:467
Async XLA Ops:
  0.0 2.5 %collective-permute-start = (f32[2,512,128]{2,1,0:T(8,128)}, f32[2,512,128]{2,1,0:T(8,128)S(1)}, u32[]{:S(2)}, u32[]{:S(2)}) collective-permute-start(f32[2,512,128]{2,1,0:T(8,128)} %data_hbm.1), channel_id=1, source_target_pairs={{0,1},{1,0},{2,3},{3,2},{4,5},{5,4},{6,7},{7,6},{8,9},{9,8},{10,11... | collective-permute-start | bytes 1572872 | tf_op jit(solution)/shard_map/ppermute | solution.py:417
